TPU v7x, 32 devices: a whole 2x2x4 slice. The times are simulated.
32 devices in a mesh: dp: 2 (over core), row: 4 (over y, x), col: 4 (over z).
Axes of the slice: x: 2, y: 2, z: 4, core: 2. Of those that a mesh axis runs over, the one named last changes fastest.
Arguments:
- tokens: bfloat16 [768, 8192], P('row', ('dp', 'col')), may hold values from -6 to 6
- prefix: int32 [8], P(('dp', 'row')), may hold values from 102 to 512, as said below
- ln1_gain: float32 [768], replicated, may hold values from 0.5 to 1.5
- ln1_bias: float32 [768], replicated, may hold values from -3 to 3
- w_qkv: bfloat16 [3, 768, 768], P(None, 'row', 'col'), may hold values from -0.21875 to 0.21875
- qv_bias: float32 [2, 768], replicated, may hold values from -3 to 3
- w_out: bfloat16 [768, 768], P('col', 'row'), may hold values from -0.875 to 0.875
- out_bias: float32 [768], replicated, may hold values from -3 to 3
- ln2_gain: float32 [768], replicated, may hold values from 0.5 to 1.5
- ln2_bias: float32 [768], replicated, may hold values from -3 to 3
- w_fc: bfloat16 [768, 3072], P('row', 'col'), may hold values from -0.21875 to 0.21875
- fc_bias: float32 [3072], replicated, may hold values from -3 to 3
- w_proj: bfloat16 [768, 3072], P('row', 'col'), may hold values from -0.109375 to 0.109375
- proj_bias: float32 [768], replicated, may hold values from -3 to 3
- cotangent: bfloat16 [768, 8192], P('row', ('dp', 'col')), may hold values from -6 to 6
Outputs:
- output: bfloat16 [768, 8192], P('row', ('dp', 'col'))
- input_grad: float32 [768, 8192], P('row', ('dp', 'col'))
- ln1_gain_grad: float32 [768], replicated
- ln1_bias_grad: float32 [768], replicated
- w_qkv_grad: float32 [3, 768, 768], P(None, 'row', 'col')
- qv_bias_grad: float32 [2, 768], replicated
- w_out_grad: float32 [768, 768], P('col', 'row')
- out_bias_grad: float32 [768], replicated
- ln2_gain_grad: float32 [768], replicated
- ln2_bias_grad: float32 [768], replicated
- w_fc_grad: float32 [768, 3072], P('row', 'col')
- fc_bias_grad: float32 [3072], replicated
- w_proj_grad: float32 [768, 3072], P('row', 'col')
- proj_bias_grad: float32 [768], replicated
Inputs may be any that keep to these rules, and one draw needn't show every extreme that they name: `prefix`: in every draw some sequence has exactly 102 and some other exactly 512.
All inputs are finite; a program needn't handle non-finite values.
Results may differ from a plain program's by a relative error of at most 0.012.
Values may be sent and summed in bfloat16 or wider, within the bound.
A program may use at most 256 MiB of HBM per device.

v0:
```python
import jax
import jax.numpy as jnp
from jax import lax
from jax.sharding import PartitionSpec as P

D = 768
FF = 3072
HEAD_DIM = 64
LEN = 1024
epsilon = 1e-05
masked_score = -1e30


def feature_totals(values):
    return lax.psum(values, "row")


def column_rows(values):
    return lax.all_gather(values, "col", axis=0, tiled=True)


def row_rows(values):
    return lax.all_gather(values, "row", axis=0, tiled=True)


def summed_over_row(term_fn, row_count):
    return lax.psum_scatter(
        term_fn(jnp.int32(0), row_count * lax.axis_size("row")),
        "row",
        scatter_dimension=0,
        tiled=True,
    )


def summed_over_col(term_fn, row_count):
    return lax.psum_scatter(
        term_fn(jnp.int32(0), row_count * lax.axis_size("col")),
        "col",
        scatter_dimension=0,
        tiled=True,
    )


def take_portion(complete, position, portion_size, along):
    return lax.dynamic_slice_in_dim(complete, position * portion_size, portion_size, along)


def place_portion(portion, position, full_size, along):
    zeroed_shape = portion.shape[:along] + (full_size,) + portion.shape[along + 1 :]
    zeroed = jnp.zeros(zeroed_shape, jnp.float32)
    return lax.dynamic_update_slice_in_dim(zeroed, portion, position * portion.shape[along], along)


def gelu_tanh(values):
    return jax.nn.gelu(values, approximate=True)


def norm_forward(values, norm_gain, norm_offset, totals_fn):
    plain_sum, square_sum = totals_fn((jnp.sum(values, axis=1), jnp.sum(values * values, axis=1)))
    center = (plain_sum / D)[:, None]
    inverse = lax.rsqrt(square_sum[:, None] / D - center * center + epsilon)
    unit_rows = (values - center) * inverse
    return (unit_rows * norm_gain + norm_offset, unit_rows, inverse)


def norm_backward(grad_rows, unit_rows, inverse, norm_gain, totals_fn):
    scaled = grad_rows * norm_gain
    plain_sum, cross_sum = totals_fn((jnp.sum(scaled, axis=1), jnp.sum(scaled * unit_rows, axis=1)))
    return inverse * (scaled - (plain_sum / D)[:, None] - unit_rows * (cross_sum / D)[:, None])


def split_heads(flat_rows):
    return flat_rows.reshape(LEN, flat_rows.shape[1] // HEAD_DIM, HEAD_DIM)


def scores_of(queries, keys_block, limit_value):
    raw_scores = jnp.einsum("qhe,khe->hqk", queries, keys_block, preferred_element_type=jnp.float32)
    raw_scores = raw_scores * HEAD_DIM ** (-0.5)
    places = jnp.arange(LEN, dtype=jnp.int32)
    visible = (places[None, :] <= places[:, None]) | (places[None, :] < limit_value)
    return jnp.where(visible[None], raw_scores, masked_score)


def attend_forward(packed):
    block_rows, limit_value = packed
    queries = split_heads(block_rows[:, 0])
    keys_block = split_heads(block_rows[:, 1])
    values_block = split_heads(block_rows[:, 2])
    scores = scores_of(queries, keys_block, limit_value)
    largest = jnp.max(scores, axis=-1, keepdims=True)
    weights = jnp.exp(scores - largest)
    row_totals = jnp.sum(weights, axis=-1, keepdims=True)
    probs = (weights / row_totals).astype(jnp.bfloat16)
    mixed = jnp.einsum("hqk,khe->qhe", probs, values_block, preferred_element_type=jnp.float32)
    return (mixed.reshape(LEN, -1).astype(jnp.bfloat16), (largest + jnp.log(row_totals))[..., 0])


def attend_backward(packed):
    block_rows, limit_value, log_total, out_grad = packed
    queries = split_heads(block_rows[:, 0])
    keys_block = split_heads(block_rows[:, 1])
    values_block = split_heads(block_rows[:, 2])
    scores = scores_of(queries, keys_block, limit_value)
    probs = jnp.exp(scores - log_total[..., None])
    probs_low = probs.astype(jnp.bfloat16)
    grad_heads = split_heads(out_grad)
    weight_grad = jnp.einsum(
        "qhe,khe->hqk", grad_heads, values_block, preferred_element_type=jnp.float32
    )
    row_inner = jnp.sum(probs * weight_grad, axis=-1, keepdims=True)
    score_grad = (probs * (weight_grad - row_inner)).astype(jnp.bfloat16)
    query_grad = jnp.einsum(
        "hqk,khe->qhe", score_grad, keys_block, preferred_element_type=jnp.float32
    )
    key_grad = jnp.einsum("hqk,qhe->khe", score_grad, queries, preferred_element_type=jnp.float32)
    value_grad = jnp.einsum(
        "hqk,qhe->khe", probs_low, grad_heads, preferred_element_type=jnp.float32
    )
    score_factor = HEAD_DIM ** (-0.5)
    stacked = jnp.stack(
        [
            (query_grad * score_factor).reshape(LEN, -1),
            (key_grad * score_factor).reshape(LEN, -1),
            value_grad.reshape(LEN, -1),
        ],
        axis=1,
    )
    return stacked.astype(jnp.bfloat16)


def on_device(
    tokens,
    prefix,
    ln1_gain,
    ln1_bias,
    w_qkv,
    qv_bias,
    w_out,
    out_bias,
    ln2_gain,
    ln2_bias,
    w_fc,
    fc_bias,
    w_proj,
    proj_bias,
    cotangent,
):
    row_place = lax.axis_index("row")
    col_place = lax.axis_index("col")
    row_devices = lax.axis_size("row")
    col_devices = lax.axis_size("col")
    width_row, local_rows = tokens.shape
    width_col = w_qkv.shape[2]
    hidden_col = w_fc.shape[1]
    seq_rows = local_rows * col_devices // row_devices
    seq_count = seq_rows // LEN
    residual = tokens.T.astype(jnp.float32)
    cotangent_local = cotangent.T
    first_gain = take_portion(ln1_gain, row_place, width_row, 0)
    first_normed, first_unit, first_inverse = norm_forward(
        residual, first_gain, take_portion(ln1_bias, row_place, width_row, 0), feature_totals
    )
    first_gathered = column_rows(first_normed.astype(jnp.bfloat16))

    def qkv_term(first_row, row_count):
        return jnp.einsum("td,sde->tse", first_gathered, w_qkv, preferred_element_type=jnp.float32)

    bias_col = take_portion(qv_bias, col_place, width_col, 1)
    bias_rows = jnp.stack([bias_col[0], jnp.zeros_like(bias_col[0]), bias_col[1]])
    qkv_sum = summed_over_row(qkv_term, seq_rows)
    qkv = (qkv_sum + bias_rows).astype(jnp.bfloat16)
    blocks = qkv.reshape(seq_count, LEN, 3, width_col)
    attn_blocks, log_totals = lax.map(attend_forward, (blocks, prefix))
    attn = attn_blocks.reshape(seq_rows, width_col)
    attn_gathered = row_rows(attn)

    def out_term(first_row, row_count):
        return jnp.dot(attn_gathered, w_out, preferred_element_type=jnp.float32)

    middle = (
        residual
        + summed_over_col(out_term, local_rows)
        + take_portion(out_bias, row_place, width_row, 0)
    )
    grad_output = cotangent_local.astype(jnp.float32)
    second_gain = take_portion(ln2_gain, row_place, width_row, 0)
    second_normed, second_unit, second_inverse = norm_forward(
        middle, second_gain, take_portion(ln2_bias, row_place, width_row, 0), feature_totals
    )
    second_gathered = column_rows(second_normed.astype(jnp.bfloat16))

    def up_term(first_row, row_count):
        return jnp.dot(second_gathered, w_fc, preferred_element_type=jnp.float32)

    hidden = summed_over_row(up_term, seq_rows) + take_portion(fc_bias, col_place, hidden_col, 0)
    active, gelu_pull = jax.vjp(gelu_tanh, hidden)
    active_gathered = row_rows(active.astype(jnp.bfloat16))

    def down_term(first_row, row_count):
        return jnp.einsum("tf,df->td", active_gathered, w_proj, preferred_element_type=jnp.float32)

    final_rows = (
        middle
        + summed_over_col(down_term, local_rows)
        + take_portion(proj_bias, row_place, width_row, 0)
    )
    output = final_rows.astype(jnp.bfloat16)
    grad_gathered = column_rows(cotangent_local)
    w_proj_grad = jnp.einsum(
        "tf,td->df", active_gathered, grad_gathered, preferred_element_type=jnp.float32
    )

    def active_term(first_row, row_count):
        return jnp.einsum("td,df->tf", grad_gathered, w_proj, preferred_element_type=jnp.float32)

    hidden_grad = gelu_pull(summed_over_row(active_term, seq_rows))[0].astype(jnp.bfloat16)
    hidden_gathered = row_rows(hidden_grad)
    w_fc_grad = jnp.einsum(
        "td,tf->df", second_gathered, hidden_gathered, preferred_element_type=jnp.float32
    )

    def second_term(first_row, row_count):
        return jnp.einsum("tf,df->td", hidden_gathered, w_fc, preferred_element_type=jnp.float32)

    second_grad = summed_over_col(second_term, local_rows)
    middle_grad = grad_output + norm_backward(
        second_grad, second_unit, second_inverse, second_gain, feature_totals
    )
    ln2_gain_part = place_portion(jnp.sum(second_grad * second_unit, axis=0), row_place, D, 0)
    ln2_bias_part = place_portion(jnp.sum(second_grad, axis=0), row_place, D, 0)
    fc_bias_part = place_portion(jnp.sum(hidden_grad.astype(jnp.float32), axis=0), col_place, FF, 0)
    proj_bias_part = place_portion(jnp.sum(grad_output, axis=0), row_place, D, 0)
    branch_grad = middle_grad.astype(jnp.bfloat16)
    branch_gathered = column_rows(branch_grad)
    w_out_grad = jnp.einsum(
        "te,td->ed", attn_gathered, branch_gathered, preferred_element_type=jnp.float32
    )

    def attn_term(first_row, row_count):
        return jnp.einsum("td,ed->te", branch_gathered, w_out, preferred_element_type=jnp.float32)

    attn_grad = summed_over_row(attn_term, seq_rows).astype(jnp.bfloat16)
    qkv_grad = lax.map(
        attend_backward, (blocks, prefix, log_totals, attn_grad.reshape(seq_count, LEN, width_col))
    )
    qkv_grad = qkv_grad.reshape(seq_rows, 3, width_col)
    qkv_gathered = row_rows(qkv_grad)
    w_qkv_grad = jnp.einsum(
        "td,tse->sde", first_gathered, qkv_gathered, preferred_element_type=jnp.float32
    )

    def first_term(first_row, row_count):
        return jnp.einsum("tse,sde->td", qkv_gathered, w_qkv, preferred_element_type=jnp.float32)

    first_grad = summed_over_col(first_term, local_rows)
    input_grad = middle_grad + norm_backward(
        first_grad, first_unit, first_inverse, first_gain, feature_totals
    )
    qkv_totals = jnp.sum(qkv_grad.astype(jnp.float32), axis=0)
    qv_part = place_portion(jnp.stack([qkv_totals[0], qkv_totals[2]]), col_place, D, 1)
    out_bias_part = place_portion(jnp.sum(branch_grad.astype(jnp.float32), axis=0), row_place, D, 0)
    ln1_gain_part = place_portion(jnp.sum(first_grad * first_unit, axis=0), row_place, D, 0)
    ln1_bias_part = place_portion(jnp.sum(first_grad, axis=0), row_place, D, 0)
    vectors = lax.psum(
        (
            ln1_gain_part,
            ln1_bias_part,
            qv_part,
            out_bias_part,
            ln2_gain_part,
            ln2_bias_part,
            fc_bias_part,
            proj_bias_part,
        ),
        ("dp", "row", "col"),
    )
    matrices = (
        lax.psum(w_qkv_grad.astype(jnp.bfloat16), "dp").astype(jnp.float32),
        lax.psum(w_out_grad.astype(jnp.bfloat16), "dp").astype(jnp.float32),
        lax.psum(w_fc_grad.astype(jnp.bfloat16), "dp").astype(jnp.float32),
        lax.psum(w_proj_grad.astype(jnp.bfloat16), "dp").astype(jnp.float32),
    )
    return (
        output.T,
        input_grad.T,
        vectors[0],
        vectors[1],
        matrices[0],
        vectors[2],
        matrices[1],
        vectors[3],
        vectors[4],
        vectors[5],
        matrices[2],
        vectors[6],
        matrices[3],
        vectors[7],
    )


def solution(mesh):
    placed = (
        P("row", ("dp", "col")),
        P(("dp", "row")),
        P(),
        P(),
        P(None, "row", "col"),
        P(),
        P("col", "row"),
        P(),
        P(),
        P(),
        P("row", "col"),
        P(),
        P("row", "col"),
        P(),
        P("row", ("dp", "col")),
    )
    return jax.shard_map(
        on_device,
        mesh=mesh,
        in_specs=placed,
        out_specs=(
            P("row", ("dp", "col")),
            P("row", ("dp", "col")),
            P(),
            P(),
            P(None, "row", "col"),
            P(),
            P("col", "row"),
            P(),
            P(),
            P(),
            P("row", "col"),
            P(),
            P("row", "col"),
            P(),
        ),
        check_vma=False,
    )
```

profile of v0, /device:TPU:0, one launch (start us, length us, event | category | flops | bytes accessed | tf_op | source)
XLA Modules:
  0.0 1165.3 jit_solution(17599242956197801233)
XLA Ops:
  11.0 11.5 all-reduce.4
  22.5 1.9 fusion.38
  25.6 35.4 %all-gather.9.cloned.1.call-done = bf16[4096,192]{0,1:T(8,128)(2,1)} async-done(((bf16[1024,192]{0,1:T(8,128)(2,1)}), bf16[4096,192]{0,1:T(8,128)(2,1)}) %all-gather.9.cloned.1.call-update) | async-done | bytes 1572880 | tf_op jit(solution)/shard_map/all_gather | solution.py:19
  61.1 6.4 fusion.61
  69.5 92.0 %reduce-scatter.9.cloned.1.call-done = f32[1024,3,192]{0,2,1:T(8,128)} async-done(((f32[4096,3,192]{0,2,1:T(8,128)}), f32[1024,3,192]{0,2,1:T(8,128)}) %reduce-scatter.9.cloned.1.call-update) | async-done | bytes 2359312 | tf_op jit(solution)/shard_map/reduce_scatter | solution.py:27
  161.5 1.9 add_convert_fusion
  163.5 3.2 fusion.55
  168.5 2.8 copy-done.2
  171.3 3.0 fusion.21
  174.4 31.1 %all-gather.11.cloned.1.call-done = bf16[4096,192]{0,1:T(8,128)(2,1)} async-done(((bf16[1024,192]{0,1:T(8,128)(2,1)}), bf16[4096,192]{0,1:T(8,128)(2,1)}) %all-gather.11.cloned.1.call-update) | async-done | bytes 1572880 | tf_op jit(solution)/shard_map/all_gather | solution.py:23
  205.5 3.7 fusion.56
  212.1 57.5 %reduce-scatter.11.cloned.1.call-done = f32[1024,192]{0,1:T(8,128)} async-done(((f32[4096,192]{0,1:T(8,128)}), f32[1024,192]{0,1:T(8,128)}) %reduce-scatter.11.cloned.1.call-update) | async-done | bytes 786448 | tf_op jit(solution)/shard_map/reduce_scatter | solution.py:36
  270.9 10.1 all-reduce.3
  282.1 26.1 %all-gather.17.cloned.1.call-done = bf16[4096,192]{0,1:T(8,128)(2,1)} async-done(((bf16[1024,192]{0,1:T(8,128)(2,1)}), bf16[4096,192]{0,1:T(8,128)(2,1)}) %all-gather.17.cloned.1.call-update) | async-done | bytes 1572880 | tf_op jit(solution)/shard_map/all_gather | solution.py:19
  308.2 7.7 fusion.59
  316.2 30.0 %all-gather.13.cloned.1.call-done = bf16[4096,192]{0,1:T(8,128)(2,1)} async-done(((bf16[1024,192]{0,1:T(8,128)(2,1)}), bf16[4096,192]{0,1:T(8,128)(2,1)}) %all-gather.13.cloned.1.call-update) | async-done | bytes 1572880 | tf_op jit(solution)/shard_map/all_gather | solution.py:19
  346.2 7.9 fusion.57
  354.9 114.0 %reduce-scatter.17.cloned.1.call-done = f32[1024,768]{1,0:T(8,128)} async-done(((f32[4096,768]{1,0:T(8,128)}), f32[1024,768]{1,0:T(8,128)}) %reduce-scatter.17.cloned.1.call-update) | async-done | bytes 3145744 | tf_op jit(solution)/shard_map/reduce_scatter | solution.py:27
  468.9 123.9 %reduce-scatter.13.cloned.1.call-done = f32[1024,768]{1,0:T(8,128)} async-done(((f32[4096,768]{1,0:T(8,128)}), f32[1024,768]{1,0:T(8,128)}) %reduce-scatter.13.cloned.1.call-update) | async-done | bytes 3145744 | tf_op jit(solution)/shard_map/reduce_scatter | solution.py:27
  592.7 5.6 convert_reduce_fusion
  598.5 70.2 %all-gather.19.cloned.1.call-done = bf16[4096,768]{1,0:T(8,128)(2,1)} async-done(((bf16[1024,768]{1,0:T(8,128)(2,1)}), bf16[4096,768]{1,0:T(8,128)(2,1)}) %all-gather.19.cloned.1.call-update) | async-done | bytes 6291472 | tf_op jit(solution)/shard_map/all_gather | solution.py:23
  668.7 6.6 fusion.60
  675.4 60.4 %reduce-scatter.19.cloned.1.call-done = f32[1024,192]{0,1:T(8,128)} async-done(((f32[4096,192]{0,1:T(8,128)}), f32[1024,192]{0,1:T(8,128)}) %reduce-scatter.19.cloned.1.call-update) | async-done | bytes 786448 | tf_op jit(solution)/shard_map/reduce_scatter | solution.py:36
  737.3 10.1 all-reduce.2
  747.3 2.2 convert_reduce_fusion.4
  749.7 35.4 %all-gather.21.cloned.1.call-done = bf16[4096,192]{0,1:T(8,128)(2,1)} async-done(((bf16[1024,192]{0,1:T(8,128)(2,1)}), bf16[4096,192]{0,1:T(8,128)(2,1)}) %all-gather.21.cloned.1.call-update) | async-done | bytes 1572880 | tf_op jit(solution)/shard_map/all_gather | solution.py:19
  785.0 3.7 fusion.62
  789.8 41.9 %reduce-scatter.21.cloned.1.call-done = f32[1024,192]{0,1:T(8,128)} async-done(((f32[4096,192]{0,1:T(8,128)}), f32[1024,192]{0,1:T(8,128)}) %reduce-scatter.21.cloned.1.call-update) | async-done | bytes 786448 | tf_op jit(solution)/shard_map/reduce_scatter | solution.py:27
  833.0 6.1 multiply_reduce_fusion
  841.8 5.2 multiply_convert_fusion
  847.0 4.2 fusion.16
  851.6 2.0 fusion.17
  853.7 2.1 fusion.18
  857.6 4.9 convolution_convert_fusion.1
  862.4 41.3 %all-gather.15.cloned.1.call-done = bf16[4096,768]{1,0:T(8,128)(2,1)} async-done(((bf16[1024,768]{1,0:T(8,128)(2,1)}), bf16[4096,768]{1,0:T(8,128)(2,1)}) %all-gather.15.cloned.1.call-update) | async-done | bytes 6291472 | tf_op jit(solution)/shard_map/all_gather | solution.py:23
  903.8 5.5 fusion.25
  910.5 52.1 %all-gather.23.cloned.1.call-done = bf16[4096,3,192]{0,2,1:T(8,128)(2,1)} async-done(((bf16[1024,3,192]{0,2,1:T(8,128)(2,1)}), bf16[4096,3,192]{0,2,1:T(8,128)(2,1)}) %all-gather.23.cloned.1.call-update) | async-done | bytes 4718608 | tf_op jit(solution)/shard_map/all_gather | solution.py:23
  962.6 5.0 fusion.26
  967.9 5.4 convolution_bitcast_fusion
  974.3 6.8 fusion.58
  983.0 4.3 all-reduce.8.cloned.1.call-done
  987.3 1.8 convert_element_type.122
  990.9 1.9 copy.34
  994.5 56.6 %reduce-scatter.23.cloned.1.call-done = f32[1024,192]{0,1:T(8,128)} async-done(((f32[4096,192]{0,1:T(8,128)}), f32[1024,192]{0,1:T(8,128)}) %reduce-scatter.23.cloned.1.call-update) | async-done | bytes 786448 | tf_op jit(solution)/shard_map/reduce_scatter | solution.py:36
  1052.5 10.1 all-reduce.1
  1062.7 51.0 %reduce-scatter.15.cloned.1.call-done = f32[1024,192]{0,1:T(8,128)} async-done(((f32[4096,192]{0,1:T(8,128)}), f32[1024,192]{0,1:T(8,128)}) %reduce-scatter.15.cloned.1.call-update) | async-done | bytes 786448 | tf_op jit(solution)/shard_map/reduce_scatter | solution.py:36
  1113.6 2.9 fusion.43
  1117.1 41.7 %all-reduce = (f32[768]{0:T(1024)}, f32[768]{0:T(1024)}, f32[2,768]{1,0:T(2,128)}, f32[768]{0:T(1024)}, f32[768]{0:T(1024)}, /*index=5*/f32[768]{0:T(1024)}, f32[3072]{0:T(1024)}, f32[768]{0:T(1024)}) all-reduce(f32[768]{0:T(1024)S(1)} %dynamic_update_slice.33, ...), channel_id=1, replica_groups=mesh['dp'=2,'row'=4,'col'=4] {'dp','row','col'}, use_global_device_ids=true, to_apply=%region_28.29 | all-reduce | flops 9216 | bytes 73728 | tf_op jit(solution)/shard_map/psum | solution.py:264
  (126 shorter events, 33.4 us)
Async XLA Ops:
  7.2 339.0 %copy-start = (bf16[192,768]{1,0:T(8,128)(2,1)S(1)}, bf16[192,768]{1,0:T(8,128)(2,1)}, u32[]{:S(2)}) copy-start(bf16[192,768]{1,0:T(8,128)(2,1)} %param.25) | copy-start | bytes 884740
  7.2 53.9 %all-gather.9.cloned.1.call-start = ((), (), s32[]{:S(2)}) async-start(), calls=%async_computation.8 | async-start | bytes 1966080 | tf_op jit(solution)/shard_map/all_gather | solution.py:19
  24.4 137.1 %reduce-scatter.9.cloned.1.call-start = ((), (), s32[]{:S(2)}) async-start(), calls=%async_computation.9 | async-start | bytes 11796480 | tf_op jit(solution)/shard_map/reduce_scatter | solution.py:27
  67.5 137.9 %all-gather.11.cloned.1.call-start = ((), (), s32[]{:S(2)}) async-start(), calls=%async_computation.10 | async-start | bytes 1966080 | tf_op jit(solution)/shard_map/all_gather | solution.py:23
  163.5 3.3 copy-start.8
  163.5 5.0 copy-start.11
  166.7 4.6 copy-start.2
  171.3 34.1 %copy-start.17 = (bf16[192,192]{1,0:T(8,128)(2,1)S(1)}, bf16[192,192]{1,0:T(8,128)(2,1)}, u32[]{:S(2)}) copy-start(bf16[192,192]{1,0:T(8,128)(2,1)} %param.21) | copy-start | bytes 221188
  174.3 95.3 %reduce-scatter.11.cloned.1.call-start = ((), (), s32[]{:S(2)}) async-start(), calls=%async_computation.11 | async-start | bytes 3932160 | tf_op jit(solution)/shard_map/reduce_scatter | solution.py:36
  209.2 60.4 %copy-start.4 = (bf16[192,1024]{1,0:T(8,128)(2,1)S(1)}, bf16[192,1024]{1,0:T(8,128)(2,1)}, u32[]{:S(2)}) copy-start(bf16[192,1024]{1,0:T(8,128)(2,1)} %param.15) | copy-start | bytes 1179652
  209.2 99.0 %copy-start.15 = (bf16[192,768]{1,0:T(8,128)(2,1)S(1)}, bf16[192,768]{1,0:T(8,128)(2,1)}, u32[]{:S(2)}) copy-start(bf16[192,768]{1,0:T(8,128)(2,1)} %param.27) | copy-start | bytes 884740
  209.2 99.0 %all-gather.17.cloned.1.call-start = ((), (), s32[]{:S(2)}) async-start(), calls=%async_computation.16 | async-start | bytes 1966080 | tf_op jit(solution)/shard_map/all_gather | solution.py:19
  209.8 136.4 %all-gather.13.cloned.1.call-start = ((), (), s32[]{:S(2)}) async-start(), calls=%async_computation.12 | async-start | bytes 1966080 | tf_op jit(solution)/shard_map/all_gather | solution.py:19
  282.0 186.9 %reduce-scatter.17.cloned.1.call-start = ((), (), s32[]{:S(2)}) async-start(), calls=%async_computation.17 | async-start | bytes 15728640 | tf_op jit(solution)/shard_map/reduce_scatter | solution.py:27
  315.9 276.8 %reduce-scatter.13.cloned.1.call-start = ((), (), s32[]{:S(2)}) async-start(), calls=%async_computation.13 | async-start | bytes 15728640 | tf_op jit(solution)/shard_map/reduce_scatter | solution.py:27
  354.0 314.7 %all-gather.19.cloned.1.call-start = ((), (), s32[]{:S(2)}) async-start(), calls=%async_computation.18 | async-start | bytes 7864320 | tf_op jit(solution)/shard_map/all_gather | solution.py:23
  598.4 137.4 %reduce-scatter.19.cloned.1.call-start = ((), (), s32[]{:S(2)}) async-start(), calls=%async_computation.19 | async-start | bytes 3932160 | tf_op jit(solution)/shard_map/reduce_scatter | solution.py:36
  675.3 72.0 %copy-start.7 = (bf16[192,1024]{1,0:T(8,128)(2,1)S(1)}, bf16[192,1024]{1,0:T(8,128)(2,1)}, u32[]{:S(2)}) copy-start(bf16[192,1024]{1,0:T(8,128)(2,1)} %param.29) | copy-start | bytes 1179652
  675.4 109.6 %all-gather.21.cloned.1.call-start = ((), (), s32[]{:S(2)}) async-start(), calls=%async_computation.20 | async-start | bytes 1966080 | tf_op jit(solution)/shard_map/all_gather | solution.py:19
  749.6 82.1 %reduce-scatter.21.cloned.1.call-start = ((), (), s32[]{:S(2)}) async-start(), calls=%async_computation.21 | async-start | bytes 3932160 | tf_op jit(solution)/shard_map/reduce_scatter | solution.py:27
  788.7 44.2 %copy-start.12 = (bf16[1024,1,192]{0,2,1:T(8,128)(2,1)S(1)}, bf16[1024,1,192]{0,2,1:T(8,128)(2,1)}, u32[]{:S(2)}) copy-start(bf16[1024,1,192]{0,2,1:T(8,128)(2,1)} %copy-done.11) | copy-start | bytes 1179652
  788.8 115.0 %all-gather.15.cloned.1.call-start = ((), (), s32[]{:S(2)}) async-start(), calls=%async_computation.14 | async-start | bytes 7864320 | tf_op jit(solution)/shard_map/all_gather | solution.py:23
  789.5 173.0 %all-gather.23.cloned.1.call-start = ((), (), s32[]{:S(2)}) async-start(), calls=%async_computation.22 | async-start | bytes 5898240 | tf_op jit(solution)/shard_map/all_gather | solution.py:23
  832.9 6.2 slice-start
  832.9 7.1 slice-start.1
  833.0 8.8 slice-start.2
  841.8 5.2 copy-start.9
  847.0 4.6 copy-start.3
  855.7 1.8 copy-start.10
  857.0 130.3 %all-reduce.8.cloned.1.call-start = ((), (), s32[]{:S(2)}) async-start(), calls=%async_computation.24 | async-start | bytes 1966080 | tf_op jit(solution)/shard_map/psum | solution.py:278
  862.4 46.8 %copy-start.6 = (bf16[4096,192]{0,1:T(8,128)(2,1)S(1)}, bf16[4096,192]{0,1:T(8,128)(2,1)}, u32[]{:S(2)}) copy-start(bf16[4096,192]{0,1:T(8,128)(2,1)} %all-gather.11.cloned.1.call-done) | copy-start | bytes 4718596
  903.8 5.5 copy-start.13
  910.5 57.4 %copy-start.14 = (bf16[3,192,192]{2,1,0:T(8,128)(2,1)S(1)}, bf16[3,192,192]{2,1,0:T(8,128)(2,1)}, u32[]{:S(2)}) copy-start(bf16[3,192,192]{2,1,0:T(8,128)(2,1)} %param.19) | copy-start | bytes 663556
  967.5 83.5 %reduce-scatter.23.cloned.1.call-start = ((), (), s32[]{:S(2)}) async-start(), calls=%async_computation.23 | async-start | bytes 3932160 | tf_op jit(solution)/shard_map/reduce_scatter | solution.py:36
  973.3 1.0 copy-start.16
  973.3 140.3 %reduce-scatter.15.cloned.1.call-start = ((), (), s32[]{:S(2)}) async-start(), calls=%async_computation.15 | async-start | bytes 3932160 | tf_op jit(solution)/shard_map/reduce_scatter | solution.py:36
  981.1 132.5 %copy-start.5 = (f32[1024,192]{0,1:T(8,128)S(1)}, f32[1024,192]{0,1:T(8,128)}, u32[]{:S(2)}) copy-start(f32[1024,192]{0,1:T(8,128)} %reduce-scatter.19.cloned.1.call-done) | copy-start | bytes 2359300
  992.8 165.9 %copy-start.1 = (bf16[192,768]{1,0:T(8,128)(2,1)S(1)}, bf16[192,768]{1,0:T(8,128)(2,1)}, u32[]{:S(2)}) copy-start(bf16[192,768]{1,0:T(8,128)(2,1)} %param.25) | copy-start | bytes 884740
Sparse Core Ops, SparseCore 0:
  24.6 36.4 all-gather.8
  67.6 93.8 reduce-scatter.8
  174.4 30.9 all-gather.10
  209.3 60.2 reduce-scatter.10
  271.0 37.1 all-gather.16
  310.2 35.9 all-gather.12
  349.3 119.5 reduce-scatter.16
  472.0 120.7 reduce-scatter.12
  598.5 70.1 all-gather.18
  675.5 60.2 reduce-scatter.18
  749.7 35.2 all-gather.20
  788.9 42.8 reduce-scatter.20
  833.6 70.1 all-gather.14
  905.5 57.0 all-gather.22
  967.7 19.5 all-reduce.7
  989.5 61.4 reduce-scatter.22
  1053.3 60.2 reduce-scatter.14
where the time goes:
time: 1170 us
  waiting for transfers between devices  924 us (79%)
  matrix products  85.4 us (7%)
  blocking collectives  83.4 us (7%)
  other arithmetic  37.2 us (3%)
  local copies, waits for them, and re-layouts  18.6 us (2%)
  between operations  15 us (1%)
    reduce_scatter x4, waiting for transfers between devices, summed_over_row(): lax.psum_scatter(term_fn(jnp.int32(0), row_count * lax.axis_size('row')),...  372 us
    reduce_scatter x4, waiting for transfers between devices, summed_over_col(): lax.psum_scatter(term_fn(jnp.int32(0), row_count * lax.axis_size('col')),...  225 us
    all_gather x4, waiting for transfers between devices, row_rows(): return lax.all_gather(values, 'row', axis=0, tiled=True)  195 us
    all_gather x4, waiting for transfers between devices, column_rows(): return lax.all_gather(values, 'col', axis=0, tiled=True)  127 us
    psum x4, blocking collectives, feature_totals(): return lax.psum(values, 'row')  41.7 us
    psum x1, blocking collectives, on_device(): lax.psum((ln1_gain_part, ln1_bias_part, qv_part, out_bias_part, ln2_gain_...  41.7 us
  transfers between devices with their start and end apart: 17, of which 17 were waited for; matrix products, arithmetic and copies ran while one was open for 7% of the time, Pallas kernels for 0%

commit v1 on v0

--- a/solution.py
+++ b/solution.py
@@ -262,17 +262,20 @@
     ln1_gain_part = place_portion(jnp.sum(first_grad * first_unit, axis=0), row_place, D, 0)
     ln1_bias_part = place_portion(jnp.sum(first_grad, axis=0), row_place, D, 0)
     vectors = lax.psum(
-        (
-            ln1_gain_part,
-            ln1_bias_part,
-            qv_part,
-            out_bias_part,
-            ln2_gain_part,
-            ln2_bias_part,
-            fc_bias_part,
-            proj_bias_part,
+        lax.psum(
+            (
+                ln1_gain_part,
+                ln1_bias_part,
+                qv_part,
+                out_bias_part,
+                ln2_gain_part,
+                ln2_bias_part,
+                fc_bias_part,
+                proj_bias_part,
+            ),
+            ("row", "col"),
         ),
-        ("dp", "row", "col"),
+        "dp",
     )
     matrices = (
         lax.psum(w_qkv_grad.astype(jnp.bfloat16), "dp").astype(jnp.float32),

time: 1170 us -> 1210 us (1.034)
  blocking collectives: 83.4 us -> 122 us
    psum x1, blocking collectives: 41.7 us -> 76.3 us  [on_device(): lax.psum((ln1_gain_part, ln1_bias_part, qv_part, out_bias_part, ln2_gain_...]
where the time goes in v1:
time: 1210 us; the launch traced here: 1200 us
  waiting for transfers between devices  924 us (76%)
  blocking collectives  122 us (10%)
  matrix products  85.4 us (7%)
  other arithmetic  37.2 us (3%)
  local copies, waits for them, and re-layouts  18.6 us (2%)
  between operations  15 us (1%)
    reduce_scatter x4, waiting for transfers between devices, summed_over_row(): lax.psum_scatter(term_fn(jnp.int32(0), row_count * lax.axis_size('row')),...  372 us
    reduce_scatter x4, waiting for transfers between devices, summed_over_col(): lax.psum_scatter(term_fn(jnp.int32(0), row_count * lax.axis_size('col')),...  225 us
    all_gather x4, waiting for transfers between devices, row_rows(): return lax.all_gather(values, 'row', axis=0, tiled=True)  195 us
    all_gather x4, waiting for transfers between devices, column_rows(): return lax.all_gather(values, 'col', axis=0, tiled=True)  127 us
    psum x1, blocking collectives, on_device(): lax.psum((ln1_gain_part, ln1_bias_part, qv_part, out_bias_part, ln2_gain_...  76.3 us
    psum x4, blocking collectives, feature_totals(): return lax.psum(values, 'row')  41.7 us
  transfers between devices with their start and end apart: 17, of which 17 were waited for; matrix products, arithmetic and copies ran while one was open for 7% of the time, Pallas kernels for 0%

profile of v1, /device:TPU:0, one launch (start us, length us, event | category | flops | bytes accessed | tf_op | source)
XLA Modules:
  0.0 1204.0 jit_solution(6226446289495670372)
XLA Ops:
  11.0 11.5 all-reduce.4
  22.5 1.9 fusion.38
  25.6 35.4 %all-gather.9.cloned.1.call-done = bf16[4096,192]{0,1:T(8,128)(2,1)} async-done(((bf16[1024,192]{0,1:T(8,128)(2,1)}), bf16[4096,192]{0,1:T(8,128)(2,1)}) %all-gather.9.cloned.1.call-update) | async-done | bytes 1572880 | tf_op jit(solution)/shard_map/all_gather | solution.py:19
  61.1 6.4 fusion.61
  69.5 92.0 %reduce-scatter.9.cloned.1.call-done = f32[1024,3,192]{0,2,1:T(8,128)} async-done(((f32[4096,3,192]{0,2,1:T(8,128)}), f32[1024,3,192]{0,2,1:T(8,128)}) %reduce-scatter.9.cloned.1.call-update) | async-done | bytes 2359312 | tf_op jit(solution)/shard_map/reduce_scatter | solution.py:27
  161.5 1.9 add_convert_fusion
  163.5 3.2 fusion.55
  168.5 2.8 copy-done.2
  171.3 3.0 fusion.21
  174.4 31.1 %all-gather.11.cloned.1.call-done = bf16[4096,192]{0,1:T(8,128)(2,1)} async-done(((bf16[1024,192]{0,1:T(8,128)(2,1)}), bf16[4096,192]{0,1:T(8,128)(2,1)}) %all-gather.11.cloned.1.call-update) | async-done | bytes 1572880 | tf_op jit(solution)/shard_map/all_gather | solution.py:23
  205.5 3.7 fusion.56
  212.1 57.5 %reduce-scatter.11.cloned.1.call-done = f32[1024,192]{0,1:T(8,128)} async-done(((f32[4096,192]{0,1:T(8,128)}), f32[1024,192]{0,1:T(8,128)}) %reduce-scatter.11.cloned.1.call-update) | async-done | bytes 786448 | tf_op jit(solution)/shard_map/reduce_scatter | solution.py:36
  270.9 10.1 all-reduce.3
  282.1 26.1 %all-gather.17.cloned.1.call-done = bf16[4096,192]{0,1:T(8,128)(2,1)} async-done(((bf16[1024,192]{0,1:T(8,128)(2,1)}), bf16[4096,192]{0,1:T(8,128)(2,1)}) %all-gather.17.cloned.1.call-update) | async-done | bytes 1572880 | tf_op jit(solution)/shard_map/all_gather | solution.py:19
  308.2 7.7 fusion.59
  316.2 30.0 %all-gather.13.cloned.1.call-done = bf16[4096,192]{0,1:T(8,128)(2,1)} async-done(((bf16[1024,192]{0,1:T(8,128)(2,1)}), bf16[4096,192]{0,1:T(8,128)(2,1)}) %all-gather.13.cloned.1.call-update) | async-done | bytes 1572880 | tf_op jit(solution)/shard_map/all_gather | solution.py:19
  346.2 7.9 fusion.57
  354.9 114.0 %reduce-scatter.17.cloned.1.call-done = f32[1024,768]{1,0:T(8,128)} async-done(((f32[4096,768]{1,0:T(8,128)}), f32[1024,768]{1,0:T(8,128)}) %reduce-scatter.17.cloned.1.call-update) | async-done | bytes 3145744 | tf_op jit(solution)/shard_map/reduce_scatter | solution.py:27
  468.9 123.9 %reduce-scatter.13.cloned.1.call-done = f32[1024,768]{1,0:T(8,128)} async-done(((f32[4096,768]{1,0:T(8,128)}), f32[1024,768]{1,0:T(8,128)}) %reduce-scatter.13.cloned.1.call-update) | async-done | bytes 3145744 | tf_op jit(solution)/shard_map/reduce_scatter | solution.py:27
  592.7 5.6 convert_reduce_fusion
  598.5 70.2 %all-gather.19.cloned.1.call-done = bf16[4096,768]{1,0:T(8,128)(2,1)} async-done(((bf16[1024,768]{1,0:T(8,128)(2,1)}), bf16[4096,768]{1,0:T(8,128)(2,1)}) %all-gather.19.cloned.1.call-update) | async-done | bytes 6291472 | tf_op jit(solution)/shard_map/all_gather | solution.py:23
  668.7 6.6 fusion.60
  675.4 60.4 %reduce-scatter.19.cloned.1.call-done = f32[1024,192]{0,1:T(8,128)} async-done(((f32[4096,192]{0,1:T(8,128)}), f32[1024,192]{0,1:T(8,128)}) %reduce-scatter.19.cloned.1.call-update) | async-done | bytes 786448 | tf_op jit(solution)/shard_map/reduce_scatter | solution.py:36
  737.3 10.1 all-reduce.2
  747.3 2.2 convert_reduce_fusion.4
  749.7 35.4 %all-gather.21.cloned.1.call-done = bf16[4096,192]{0,1:T(8,128)(2,1)} async-done(((bf16[1024,192]{0,1:T(8,128)(2,1)}), bf16[4096,192]{0,1:T(8,128)(2,1)}) %all-gather.21.cloned.1.call-update) | async-done | bytes 1572880 | tf_op jit(solution)/shard_map/all_gather | solution.py:19
  785.0 3.7 fusion.62
  789.8 41.9 %reduce-scatter.21.cloned.1.call-done = f32[1024,192]{0,1:T(8,128)} async-done(((f32[4096,192]{0,1:T(8,128)}), f32[1024,192]{0,1:T(8,128)}) %reduce-scatter.21.cloned.1.call-update) | async-done | bytes 786448 | tf_op jit(solution)/shard_map/reduce_scatter | solution.py:27
  833.0 6.1 multiply_reduce_fusion
  841.8 5.2 multiply_convert_fusion
  847.0 4.2 fusion.16
  851.6 2.0 fusion.17
  853.7 2.1 fusion.18
  857.6 4.9 convolution_convert_fusion.1
  862.4 41.3 %all-gather.15.cloned.1.call-done = bf16[4096,768]{1,0:T(8,128)(2,1)} async-done(((bf16[1024,768]{1,0:T(8,128)(2,1)}), bf16[4096,768]{1,0:T(8,128)(2,1)}) %all-gather.15.cloned.1.call-update) | async-done | bytes 6291472 | tf_op jit(solution)/shard_map/all_gather | solution.py:23
  903.8 5.5 fusion.25
  910.5 52.1 %all-gather.23.cloned.1.call-done = bf16[4096,3,192]{0,2,1:T(8,128)(2,1)} async-done(((bf16[1024,3,192]{0,2,1:T(8,128)(2,1)}), bf16[4096,3,192]{0,2,1:T(8,128)(2,1)}) %all-gather.23.cloned.1.call-update) | async-done | bytes 4718608 | tf_op jit(solution)/shard_map/all_gather | solution.py:23
  962.6 5.0 fusion.26
  967.9 5.4 convolution_bitcast_fusion
  974.3 6.8 fusion.58
  983.0 4.3 all-reduce.9.cloned.1.call-done
  990.9 1.9 copy.34
  994.5 56.6 %reduce-scatter.23.cloned.1.call-done = f32[1024,192]{0,1:T(8,128)} async-done(((f32[4096,192]{0,1:T(8,128)}), f32[1024,192]{0,1:T(8,128)}) %reduce-scatter.23.cloned.1.call-update) | async-done | bytes 786448 | tf_op jit(solution)/shard_map/reduce_scatter | solution.py:36
  1052.5 10.1 all-reduce.1
  1062.7 51.0 %reduce-scatter.15.cloned.1.call-done = f32[1024,192]{0,1:T(8,128)} async-done(((f32[4096,192]{0,1:T(8,128)}), f32[1024,192]{0,1:T(8,128)}) %reduce-scatter.15.cloned.1.call-update) | async-done | bytes 786448 | tf_op jit(solution)/shard_map/reduce_scatter | solution.py:36
  1113.6 2.9 fusion.43
  1117.1 76.3 %all-reduce = (f32[768]{0:T(1024)S(1)}, f32[768]{0:T(1024)S(1)}, f32[2,768]{1,0:T(2,128)S(1)}, f32[768]{0:T(1024)S(1)}, f32[768]{0:T(1024)S(1)}, /*index=5*/f32[...) all-reduce(f32[768]{0:T(1024)S(1)} %dynamic_update_slice.33, ...), channel_id=1, replica_groups=mesh['dp'=2,'row'=4,'col'=4] {'row','col'}, use_global_device_ids=true, to_apply=%region_28.29 | all-reduce | flops 9216 | bytes 73728 | tf_op jit(solution)/shard_map/psum | solution.py:265
  1193.4 4.1 all-reduce.5
  (127 shorter events, 35.2 us)
Async XLA Ops:
  7.2 339.0 %copy-start = (bf16[192,768]{1,0:T(8,128)(2,1)S(1)}, bf16[192,768]{1,0:T(8,128)(2,1)}, u32[]{:S(2)}) copy-start(bf16[192,768]{1,0:T(8,128)(2,1)} %param.25) | copy-start | bytes 884740
  7.2 53.9 %all-gather.9.cloned.1.call-start = ((), (), s32[]{:S(2)}) async-start(), calls=%async_computation.8 | async-start | bytes 1966080 | tf_op jit(solution)/shard_map/all_gather | solution.py:19
  24.4 137.1 %reduce-scatter.9.cloned.1.call-start = ((), (), s32[]{:S(2)}) async-start(), calls=%async_computation.9 | async-start | bytes 11796480 | tf_op jit(solution)/shard_map/reduce_scatter | solution.py:27
  67.5 137.9 %all-gather.11.cloned.1.call-start = ((), (), s32[]{:S(2)}) async-start(), calls=%async_computation.10 | async-start | bytes 1966080 | tf_op jit(solution)/shard_map/all_gather | solution.py:23
  163.5 3.3 copy-start.8
  163.5 5.0 copy-start.11
  166.7 4.6 copy-start.2
  171.3 34.1 %copy-start.17 = (bf16[192,192]{1,0:T(8,128)(2,1)S(1)}, bf16[192,192]{1,0:T(8,128)(2,1)}, u32[]{:S(2)}) copy-start(bf16[192,192]{1,0:T(8,128)(2,1)} %param.21) | copy-start | bytes 221188
  174.3 95.3 %reduce-scatter.11.cloned.1.call-start = ((), (), s32[]{:S(2)}) async-start(), calls=%async_computation.11 | async-start | bytes 3932160 | tf_op jit(solution)/shard_map/reduce_scatter | solution.py:36
  209.2 60.4 %copy-start.4 = (bf16[192,1024]{1,0:T(8,128)(2,1)S(1)}, bf16[192,1024]{1,0:T(8,128)(2,1)}, u32[]{:S(2)}) copy-start(bf16[192,1024]{1,0:T(8,128)(2,1)} %param.15) | copy-start | bytes 1179652
  209.2 99.0 %copy-start.15 = (bf16[192,768]{1,0:T(8,128)(2,1)S(1)}, bf16[192,768]{1,0:T(8,128)(2,1)}, u32[]{:S(2)}) copy-start(bf16[192,768]{1,0:T(8,128)(2,1)} %param.27) | copy-start | bytes 884740
  209.2 99.0 %all-gather.17.cloned.1.call-start = ((), (), s32[]{:S(2)}) async-start(), calls=%async_computation.16 | async-start | bytes 1966080 | tf_op jit(solution)/shard_map/all_gather | solution.py:19
  209.8 136.4 %all-gather.13.cloned.1.call-start = ((), (), s32[]{:S(2)}) async-start(), calls=%async_computation.12 | async-start | bytes 1966080 | tf_op jit(solution)/shard_map/all_gather | solution.py:19
  282.0 186.9 %reduce-scatter.17.cloned.1.call-start = ((), (), s32[]{:S(2)}) async-start(), calls=%async_computation.17 | async-start | bytes 15728640 | tf_op jit(solution)/shard_map/reduce_scatter | solution.py:27
  315.9 276.8 %reduce-scatter.13.cloned.1.call-start = ((), (), s32[]{:S(2)}) async-start(), calls=%async_computation.13 | async-start | bytes 15728640 | tf_op jit(solution)/shard_map/reduce_scatter | solution.py:27
  354.0 314.7 %all-gather.19.cloned.1.call-start = ((), (), s32[]{:S(2)}) async-start(), calls=%async_computation.18 | async-start | bytes 7864320 | tf_op jit(solution)/shard_map/all_gather | solution.py:23
  598.4 137.4 %reduce-scatter.19.cloned.1.call-start = ((), (), s32[]{:S(2)}) async-start(), calls=%async_computation.19 | async-start | bytes 3932160 | tf_op jit(solution)/shard_map/reduce_scatter | solution.py:36
  675.3 72.0 %copy-start.7 = (bf16[192,1024]{1,0:T(8,128)(2,1)S(1)}, bf16[192,1024]{1,0:T(8,128)(2,1)}, u32[]{:S(2)}) copy-start(bf16[192,1024]{1,0:T(8,128)(2,1)} %param.29) | copy-start | bytes 1179652
  675.4 109.6 %all-gather.21.cloned.1.call-start = ((), (), s32[]{:S(2)}) async-start(), calls=%async_computation.20 | async-start | bytes 1966080 | tf_op jit(solution)/shard_map/all_gather | solution.py:19
  749.6 82.1 %reduce-scatter.21.cloned.1.call-start = ((), (), s32[]{:S(2)}) async-start(), calls=%async_computation.21 | async-start | bytes 3932160 | tf_op jit(solution)/shard_map/reduce_scatter | solution.py:27
  788.7 44.2 %copy-start.12 = (bf16[1024,1,192]{0,2,1:T(8,128)(2,1)S(1)}, bf16[1024,1,192]{0,2,1:T(8,128)(2,1)}, u32[]{:S(2)}) copy-start(bf16[1024,1,192]{0,2,1:T(8,128)(2,1)} %copy-done.11) | copy-start | bytes 1179652
  788.8 115.0 %all-gather.15.cloned.1.call-start = ((), (), s32[]{:S(2)}) async-start(), calls=%async_computation.14 | async-start | bytes 7864320 | tf_op jit(solution)/shard_map/all_gather | solution.py:23
  789.5 173.0 %all-gather.23.cloned.1.call-start = ((), (), s32[]{:S(2)}) async-start(), calls=%async_computation.22 | async-start | bytes 5898240 | tf_op jit(solution)/shard_map/all_gather | solution.py:23
  832.9 6.2 slice-start
  832.9 7.1 slice-start.1
  833.0 8.8 slice-start.2
  841.8 5.2 copy-start.9
  847.0 4.6 copy-start.3
  855.7 1.8 copy-start.10
  857.0 130.3 %all-reduce.9.cloned.1.call-start = ((), (), s32[]{:S(2)}) async-start(), calls=%async_computation.24 | async-start | bytes 1966080 | tf_op jit(solution)/shard_map/psum | solution.py:281
  862.4 46.8 %copy-start.6 = (bf16[4096,192]{0,1:T(8,128)(2,1)S(1)}, bf16[4096,192]{0,1:T(8,128)(2,1)}, u32[]{:S(2)}) copy-start(bf16[4096,192]{0,1:T(8,128)(2,1)} %all-gather.11.cloned.1.call-done) | copy-start | bytes 4718596
  903.8 5.5 copy-start.13
  910.5 57.4 %copy-start.14 = (bf16[3,192,192]{2,1,0:T(8,128)(2,1)S(1)}, bf16[3,192,192]{2,1,0:T(8,128)(2,1)}, u32[]{:S(2)}) copy-start(bf16[3,192,192]{2,1,0:T(8,128)(2,1)} %param.19) | copy-start | bytes 663556
  967.5 83.5 %reduce-scatter.23.cloned.1.call-start = ((), (), s32[]{:S(2)}) async-start(), calls=%async_computation.23 | async-start | bytes 3932160 | tf_op jit(solution)/shard_map/reduce_scatter | solution.py:36
  973.3 1.0 copy-start.16
  973.3 140.3 %reduce-scatter.15.cloned.1.call-start = ((), (), s32[]{:S(2)}) async-start(), calls=%async_computation.15 | async-start | bytes 3932160 | tf_op jit(solution)/shard_map/reduce_scatter | solution.py:36
  981.1 132.5 %copy-start.5 = (f32[1024,192]{0,1:T(8,128)S(1)}, f32[1024,192]{0,1:T(8,128)}, u32[]{:S(2)}) copy-start(f32[1024,192]{0,1:T(8,128)} %reduce-scatter.19.cloned.1.call-done) | copy-start | bytes 2359300
  992.8 204.6 %copy-start.1 = (bf16[192,768]{1,0:T(8,128)(2,1)S(1)}, bf16[192,768]{1,0:T(8,128)(2,1)}, u32[]{:S(2)}) copy-start(bf16[192,768]{1,0:T(8,128)(2,1)} %param.25) | copy-start | bytes 884740
Sparse Core Ops, SparseCore 0:
  24.6 36.4 all-gather.8
  67.6 93.8 reduce-scatter.8
  174.4 30.9 all-gather.10
  209.3 60.2 reduce-scatter.10
  271.0 37.1 all-gather.16
  310.2 35.9 all-gather.12
  349.3 119.5 reduce-scatter.16
  472.0 120.7 reduce-scatter.12
  598.5 70.1 all-gather.18
  675.5 60.2 reduce-scatter.18
  749.7 35.2 all-gather.20
  788.9 42.8 reduce-scatter.20
  833.6 70.1 all-gather.14
  905.5 57.0 all-gather.22
  967.7 19.5 all-reduce.8
  989.5 61.4 reduce-scatter.22
  1053.3 60.2 reduce-scatter.14
